TPU v7x, 256 devices: a whole 4x4x8 slice. The times are simulated.
256 devices in a mesh: section: 2 (over z_lo), fsdp: 32 (over z_hi, y, core), tensor: 4 (over x).
Axes of the slice: x: 4, y: 4, z: 8 (z_hi: 4, z_lo: 2; z = z_hi * 2 + z_lo), core: 2. Of those that a mesh axis runs over, the one named last changes fastest.
Arguments:
- frames: bfloat16 [4096, 3072], P('fsdp', 'tensor')
- lengths: int32 [32], P('fsdp'), may hold values from 16 to 128, as said below
- qkv_weight: bfloat16 [2, 3, 3072, 1536], P('section', None, 'fsdp', 'tensor'), as said below
- out_weight: bfloat16 [2, 1536, 3072], P('section', 'tensor', 'fsdp'), may hold values from -0.15625 to 0.15625
- grad_out: bfloat16 [4096, 3072], P('fsdp', 'tensor'), may hold values from -6 to 6
Outputs:
- input_grads: bfloat16 [2, 4096, 3072], P('section', 'fsdp', 'tensor')
- qkv_grad: bfloat16 [2, 3, 3072, 1536], P('section', None, 'fsdp', 'tensor')
- out_grad: bfloat16 [2, 1536, 3072], P('section', 'tensor', 'fsdp')
Inputs may be any that keep to these rules, and one draw needn't show every extreme that they name: Utterance b's live frames are its first lengths[b] slots; some utterance fills all 128 slots. `qkv_weight`: index 0, 1, 2 of the second dimension are the query, key and value projections.
All inputs are finite; a program needn't handle non-finite values.
Results may differ from a plain program's by a relative error of at most 0.03.
Values may be sent and summed in bfloat16 or wider, within the bound.
No kernel may reach another device: no remote copies, remote signals or barrier semaphores. Data moves between devices by JAX's collectives and lax.ppermute only.
A program may use at most 64 MiB of HBM per device.

v0:
```python
import jax
import jax.numpy as jnp
from jax import lax
from jax.sharding import PartitionSpec as P

HEAD = 128
EPSILON = 1e-05


def from_behind(value, axis, steps):
    count = lax.axis_size(axis)
    leading, last = (max(0, -steps), min(count, count - steps))
    return lax.ppermute(value, axis, [(source, source + steps) for source in range(leading, last)])


def attend_forward(queries, key_rows, values, live_keys):
    score_scale = float(HEAD) ** (-0.5)
    scores = (
        jnp.einsum("bqhe,bkhe->bhqk", queries, key_rows, preferred_element_type=jnp.float32)
        * score_scale
    )
    scores = jnp.where(live_keys[:, None, None, :], scores, jnp.float32(-1e30))
    highest = jnp.max(scores, axis=-1, keepdims=True)
    raised = jnp.exp(scores - highest)
    attend = raised / jnp.sum(raised, axis=-1, keepdims=True)
    attend_low = attend.astype(jnp.bfloat16)
    context = jnp.einsum(
        "bhqk,bkhe->bqhe", attend_low, values, preferred_element_type=jnp.float32
    ).astype(jnp.bfloat16)
    return (attend, attend_low, context)


def layer_forward(hidden_own, w_qkv, w_out, live_keys, live_rows):
    whole = lax.all_gather(hidden_own, "tensor", axis=1, tiled=True)
    widened = whole.astype(jnp.float32)
    average = jnp.mean(widened, axis=-1, keepdims=True)
    centered = widened - average
    variance = jnp.mean(centered * centered, axis=-1, keepdims=True)
    inverse = lax.rsqrt(variance + EPSILON)
    unit_rows = centered * inverse
    normed = unit_rows.astype(jnp.bfloat16)
    projected = jnp.einsum("rd,cdh->crh", normed, w_qkv, preferred_element_type=jnp.float32).astype(
        jnp.bfloat16
    )
    utterances, length = live_keys.shape
    split_qkv = projected.reshape(3, utterances, length, -1, HEAD)
    attend, attend_low, context = attend_forward(
        split_qkv[0], split_qkv[1], split_qkv[2], live_keys
    )
    context = context.reshape(utterances * length, -1)
    mixed = jnp.dot(context, w_out, preferred_element_type=jnp.float32)
    mixed_own = lax.psum_scatter(mixed, "tensor", scatter_dimension=1, tiled=True)
    output = (hidden_own.astype(jnp.float32) + live_rows * mixed_own).astype(jnp.bfloat16)
    return (output, (unit_rows, inverse, normed, split_qkv, attend, attend_low, context))


def layer_backward(grad_own, kept_state, w_qkv, w_out, live_rows):
    unit_rows, inverse, normed, split_qkv, attend, attend_low, context = kept_state
    score_scale = float(HEAD) ** (-0.5)
    whole_grad = lax.all_gather(grad_own, "tensor", axis=1, tiled=True)
    masked = (live_rows * whole_grad.astype(jnp.float32)).astype(jnp.bfloat16)
    grad_context = jnp.einsum(
        "rd,hd->rh", masked, w_out, preferred_element_type=jnp.float32
    ).astype(jnp.bfloat16)
    grad_context = grad_context.reshape(split_qkv.shape[1:])
    queries, key_rows, values = (split_qkv[0], split_qkv[1], split_qkv[2])
    grad_attend = jnp.einsum(
        "bqhe,bkhe->bhqk", grad_context, values, preferred_element_type=jnp.float32
    )
    grad_values = jnp.einsum(
        "bhqk,bqhe->bkhe", attend_low, grad_context, preferred_element_type=jnp.float32
    ).astype(jnp.bfloat16)
    inner = jnp.sum(grad_attend * attend, axis=-1, keepdims=True)
    grad_scores = (attend * (grad_attend - inner) * score_scale).astype(jnp.bfloat16)
    grad_queries = jnp.einsum(
        "bhqk,bkhe->bqhe", grad_scores, key_rows, preferred_element_type=jnp.float32
    ).astype(jnp.bfloat16)
    grad_keys = jnp.einsum(
        "bhqk,bqhe->bkhe", grad_scores, queries, preferred_element_type=jnp.float32
    ).astype(jnp.bfloat16)
    frame_rows, own_width = grad_own.shape
    grad_qkv = jnp.stack([grad_queries, grad_keys, grad_values]).reshape(3, frame_rows, -1)
    norm_part = jnp.einsum("crh,cdh->rd", grad_qkv, w_qkv, preferred_element_type=jnp.float32)
    first_col = lax.axis_index("tensor") * own_width
    norm_grad = lax.psum(norm_part.astype(jnp.bfloat16), "tensor").astype(jnp.float32)
    centered = (
        norm_grad
        - jnp.mean(norm_grad, axis=-1, keepdims=True)
        - unit_rows * jnp.mean(norm_grad * unit_rows, axis=-1, keepdims=True)
    )
    centered_own = lax.dynamic_slice_in_dim(centered, first_col, own_width, 1)
    grad_in = (grad_own.astype(jnp.float32) + inverse * centered_own).astype(jnp.bfloat16)
    return (grad_in, masked, grad_qkv)


def local(frames, lengths, qkv_weight, out_weight, grad_out):
    frame_rows = frames.shape[0]
    utterances = lengths.shape[0]
    length = frame_rows // utterances
    live_keys = jnp.arange(length, dtype=jnp.int32)[None, :] < lengths[:, None]
    live_rows = live_keys.reshape(frame_rows, 1).astype(jnp.float32)
    gathered = (
        lax.all_gather(qkv_weight, "fsdp", axis=2, tiled=True),
        lax.all_gather(out_weight, "fsdp", axis=2, tiled=True),
    )
    w_qkv = gathered[0][0]
    w_out = gathered[1][0]
    first_out, _ = layer_forward(frames, w_qkv, w_out, live_keys, live_rows)
    arrived = from_behind(first_out, "section", 1)
    on_first = lax.axis_index("section") == 0
    entry = jnp.where(on_first, frames, arrived)
    _, kept_state = layer_forward(entry, w_qkv, w_out, live_keys, live_rows)
    upper_grad, _, _ = layer_backward(grad_out, kept_state, w_qkv, w_out, live_rows)
    returned = from_behind(upper_grad, "section", -1)
    top_grad = jnp.where(on_first, returned, grad_out)
    grad_in, masked, grad_qkv = layer_backward(top_grad, kept_state, w_qkv, w_out, live_rows)
    normed = kept_state[2]
    context = kept_state[6]
    full_width = normed.shape[1]
    head_width = context.shape[1]
    term_qkv = jnp.einsum(
        "rd,crh->dch", normed, grad_qkv, preferred_element_type=jnp.float32
    ).reshape(full_width, 3 * head_width)
    term_out = jnp.einsum("rd,rh->dh", masked, context, preferred_element_type=jnp.float32)
    summed = lax.psum_scatter(
        jnp.concatenate([term_qkv, term_out], axis=1).astype(jnp.bfloat16),
        "fsdp",
        scatter_dimension=0,
        tiled=True,
    ).astype(jnp.float32)
    own_rows = summed.shape[0]
    qkv_grad = (
        summed[:, : 3 * head_width]
        .reshape(own_rows, 3, head_width)
        .transpose(1, 0, 2)[None]
        .astype(jnp.bfloat16)
    )
    out_grad = summed[:, 3 * head_width :].T[None].astype(jnp.bfloat16)
    return (grad_in[None], qkv_grad, out_grad)


def solution(mesh):
    in_specs = (
        P("fsdp", "tensor"),
        P("fsdp"),
        P("section", None, "fsdp", "tensor"),
        P("section", "tensor", "fsdp"),
        P("fsdp", "tensor"),
    )
    out_specs = (
        P("section", "fsdp", "tensor"),
        P("section", None, "fsdp", "tensor"),
        P("section", "tensor", "fsdp"),
    )
    return jax.shard_map(local, mesh=mesh, in_specs=in_specs, out_specs=out_specs, check_vma=False)
```

profile of v0, /device:TPU:1, one launch (start us, length us, event | category | flops | bytes accessed | tf_op | source)
XLA Modules:
  0.0 505.9 jit_solution(2395847243303926381)
XLA Ops:
  9.4 13.1 %all_gather.18 = bf16[128,3072]{1,0:T(8,128)(2,1)S(1)} all-gather(bf16[128,768]{1,0:T(8,128)(2,1)} %param.5), channel_id=1, replica_groups=mesh['section'=2,'fsdp'=32,'tensor'=4] {'tensor'}, dimensions={1}, use_global_device_ids=true | all-gather | bytes 983040 | tf_op jit(solution)/shard_map/all_gather | solution.py:34
  23.1 64.4 %all-gather.3.cloned.1.call-done = bf16[1,3,3072,384]{3,2,1,0:T(8,128)(2,1)} async-done(((bf16[1,3,96,384]{3,2,1,0:T(8,128)(2,1)}), bf16[1,3,3072,384]{3,2,1,0:T(8,128)(2,1)}) %all-gather.3.cloned.1.call-update) | async-done | bytes 7077904 | tf_op jit(solution)/shard_map/all_gather | solution.py:103
  87.4 4.2 fusion.48
  92.8 50.7 %all-gather.5.cloned.1.call-done = bf16[1,384,3072]{1,2,0:T(8,128)(2,1)} async-done(((bf16[1,384,96]{1,2,0:T(8,128)(2,1)}), bf16[1,384,3072]{1,2,0:T(8,128)(2,1)}) %all-gather.5.cloned.1.call-update) | async-done | bytes 2359312 | tf_op jit(solution)/shard_map/all_gather | solution.py:104
  143.5 3.7 fusion.28
  148.2 14.8 %all_gather.22 = bf16[128,3072]{1,0:T(8,128)(2,1)S(1)} all-gather(bf16[128,768]{1,0:T(8,128)(2,1)S(1)} %copy-done.6), channel_id=1, replica_groups=mesh['section'=2,'fsdp'=32,'tensor'=4] {'tensor'}, dimensions={1}, use_global_device_ids=true | all-gather | bytes 983040 | tf_op jit(solution)/shard_map/all_gather | solution.py:60
  163.0 11.8 %reduce-scatter.5.cloned.1.call-done = f32[128,768]{1,0:T(8,128)} async-done(((f32[128,3072]{1,0:T(8,128)}), f32[128,768]{1,0:T(8,128)}) %reduce-scatter.5.cloned.1.call-update) | async-done | bytes 393232 | tf_op jit(solution)/shard_map/reduce_scatter | solution.py:52
  176.6 2.0 collective-permute-start
  181.5 12.3 %all_gather.21 = bf16[128,3072]{1,0:T(8,128)(2,1)S(1)} all-gather(bf16[128,768]{1,0:T(8,128)(2,1)S(1)} %broadcast_select_fusion.1), channel_id=1, replica_groups=mesh['section'=2,'fsdp'=32,'tensor'=4] {'tensor'}, dimensions={1}, use_global_device_ids=true | all-gather | bytes 983040 | tf_op jit(solution)/shard_map/all_gather | solution.py:34
  194.4 4.2 fusion.45
  204.6 2.5 fusion.125
  207.1 2.1 convolution_convert_fusion.6
  209.1 2.1 convolution_convert_fusion.8
  211.3 2.1 convolution_convert_fusion.7
  217.7 6.4 %fusion.21 = bf16[128,3072]{1,0:T(8,128)(2,1)} fusion(bf16[1,3,3072,384]{3,2,1,0:T(8,128)(2,1)} %all-gather.3.cloned.1.call-done, bf16[1,128,384]{2,1,0:T(8,128)(2,1)S(1)} %copy.92, bf16[1,128,384]{2,1,0:T(8,128)(2,1)} %copy.91, bf16[1,128,384]{2,1,0:T(8,128)(2,1)} %copy.90), kind=kOutput, calls=%fused_computation.18 | convolution fusion | flops 906657792 | bytes 8159232 | tf_op jit(solution)/shard_map/crh,cdh->rd/dot_general | solution.py:83
  224.2 50.4 %all-reduce.3.cloned.1.call-done = bf16[128,3072]{1,0:T(8,128)(2,1)} async-done(((bf16[128,3072]{1,0:T(8,128)(2,1)}), bf16[128,3072]{1,0:T(8,128)(2,1)}) %all-reduce.3.cloned.1.call-update) | async-done | bytes 786448 | tf_op jit(solution)/shard_map/psum | solution.py:85
  280.9 3.5 collective-permute-done.1
  285.3 10.7 %all_gather.23 = bf16[128,3072]{1,0:T(8,128)(2,1)S(1)} all-gather(bf16[128,768]{1,0:T(8,128)(2,1)S(1)} %broadcast_select_fusion), channel_id=1, replica_groups=mesh['section'=2,'fsdp'=32,'tensor'=4] {'tensor'}, dimensions={1}, use_global_device_ids=true | all-gather | bytes 983040 | tf_op jit(solution)/shard_map/all_gather | solution.py:60
  302.5 6.3 %fusion.18 = bf16[128,3072]{1,0:T(8,128)(2,1)} fusion(bf16[1,3,3072,384]{3,2,1,0:T(8,128)(2,1)} %all-gather.3.cloned.1.call-done, bf16[1,128,384]{2,1,0:T(8,128)(2,1)S(1)} %copy.101, bf16[1,128,384]{2,1,0:T(8,128)(2,1)S(1)} %copy.100, bf16[1,128,384]{2,1,0:T(8,128)(2,1)S(1)} %copy.99), kind=kOutput, calls=%fused_computation.17 | convolution fusion | flops 906657792 | bytes 8159232 | tf_op jit(solution)/shard_map/crh,cdh->rd/dot_general | solution.py:83
  309.7 2.1 convolution_convert_fusion
  311.8 10.1 %pad_maximum_fusion = bf16[3072,1536]{0,1:T(8,128)(2,1)} fusion(bf16[3072,384]{0,1:T(8,128)(2,1)S(1)} %convolution_convert_fusion.1, bf16[3072,1152]{0,1:T(8,128)(2,1)S(1)} %convolution_convert_fusion), kind=kLoop, calls=%fused_computation.5 | loop fusion | flops 18874368 | bytes 18874368 | tf_op jit(solution)/shard_map/concatenate | solution.py:126
  322.0 12.7 %copy.122 = bf16[3072,1536]{1,0:T(8,128)(2,1)} copy(bf16[3072,1536]{0,1:T(8,128)(2,1)} %pad_maximum_fusion) | data formatting | bytes 18874368
  334.7 28.0 %all-reduce.5.cloned.1.call-done = bf16[128,3072]{1,0:T(8,128)(2,1)} async-done(((bf16[128,3072]{1,0:T(8,128)(2,1)}), bf16[128,3072]{1,0:T(8,128)(2,1)}) %all-reduce.5.cloned.1.call-update) | async-done | bytes 786448 | tf_op jit(solution)/shard_map/psum | solution.py:85
  366.5 128.8 %reduce-scatter.7.cloned.1.call-done = bf16[96,1536]{1,0:T(8,128)(2,1)} async-done(((bf16[3072,1536]{1,0:T(8,128)(2,1)}), bf16[96,1536]{1,0:T(8,128)(2,1)}) %reduce-scatter.7.cloned.1.call-update) | async-done | bytes 294928
  (104 shorter events, 41.7 us)
Async XLA Ops:
  7.2 80.3 %all-gather.3.cloned.1.call-start = ((), (), s32[]{:S(2)}) async-start(), calls=%async_computation.2 | async-start | bytes 7299072 | tf_op jit(solution)/shard_map/all_gather | solution.py:103
  7.9 135.6 %all-gather.5.cloned.1.call-start = ((), (), s32[]{:S(2)}) async-start(), calls=%async_computation.3 | async-start | bytes 2433024 | tf_op jit(solution)/shard_map/all_gather | solution.py:104
  8.6 166.1 %reduce-scatter.5.cloned.1.call-start = ((), (), s32[]{:S(2)}) async-start(), calls=%async_computation.4 | async-start | bytes 1966080 | tf_op jit(solution)/shard_map/reduce_scatter | solution.py:52
  147.2 0.9 copy-start.6
  147.2 27.6 %copy-start.7 = (bf16[128,768]{1,0:T(8,128)(2,1)S(1)}, bf16[128,768]{1,0:T(8,128)(2,1)}, u32[]{:S(2)}) copy-start(bf16[128,768]{1,0:T(8,128)(2,1)} %param.5) | copy-start | bytes 589828
  147.3 31.3 %copy-start = (bf16[1,384,3072]{1,2,0:T(8,128)(2,1)S(1)}, bf16[1,384,3072]{1,2,0:T(8,128)(2,1)}, u32[]{:S(2)}) copy-start(bf16[1,384,3072]{1,2,0:T(8,128)(2,1)} %all-gather.5.cloned.1.call-done) | copy-start | bytes 7077892
  147.3 127.3 %all-reduce.3.cloned.1.call-start = ((), (), s32[]{:S(2)}) async-start(), calls=%async_computation.5 | async-start | bytes 1572864 | tf_op jit(solution)/shard_map/psum | solution.py:85
  176.6 4.9 collective-permute-start
  200.4 78.5 %copy-start.8 = (bf16[1,128,384]{1,2,0:T(8,128)(2,1)}, bf16[1,128,384]{1,2,0:T(8,128)(2,1)S(1)}, u32[]{:S(2)}) copy-start(bf16[1,128,384]{1,2,0:T(8,128)(2,1)S(1)} %copy.84) | copy-start | bytes 294916
  202.8 8.5 %copy-start.11 = (bf16[1,128,384]{1,2,0:T(8,128)(2,1)S(1)}, bf16[1,128,384]{1,2,0:T(8,128)(2,1)}, u32[]{:S(2)}) copy-start(bf16[1,128,384]{1,2,0:T(8,128)(2,1)} %copy.80) | copy-start | bytes 294916
  224.1 138.6 %all-reduce.5.cloned.1.call-start = ((), (), s32[]{:S(2)}) async-start(), calls=%async_computation.6 | async-start | bytes 1572864 | tf_op jit(solution)/shard_map/psum | solution.py:85
  274.6 1.8 copy-start.5
  276.4 1.2 copy-start.3
  276.4 2.5 copy-start.12
  277.6 6.7 %collective-permute-start.1 = (bf16[128,768]{1,0:T(8,128)(2,1)}, bf16[128,768]{1,0:T(8,128)(2,1)}, u32[]{:S(2)}, u32[]{:S(2)}) collective-permute-start(bf16[128,768]{1,0:T(8,128)(2,1)} %fusion.82), channel_id=1, source_target_pairs={{128,0},{129,1},{130,2},{131,3},{132,4},{133,5},{134,6},{135,7},{1... | collective-permute-start | bytes 589832 | tf_op jit(solution)/shard_map/ppermute | solution.py:13
  295.9 0.9 copy-start.1
  296.8 2.2 copy-start.9
  297.4 1.8 copy-start.14
  297.5 1.8 copy-start.15
  297.5 3.0 copy-start.13
  302.4 6.4 %copy-start.2 = (bf16[128,3072]{1,0:T(8,128)(2,1)S(1)}, bf16[128,3072]{1,0:T(8,128)(2,1)}, u32[]{:S(2)}) copy-start(bf16[128,3072]{1,0:T(8,128)(2,1)} %copy-done.1) | copy-start | bytes 2359300
  302.4 6.4 %copy-start.10 = (bf16[3,128,128]{2,1,0:T(8,128)(2,1)S(1)}, bf16[3,128,128]{2,1,0:T(8,128)(2,1)}, u32[]{:S(2)}) copy-start(bf16[3,128,128]{2,1,0:T(8,128)(2,1)} %convolution_convert_fusion.2) | copy-start | bytes 294916
  308.8 186.5 %reduce-scatter.7.cloned.1.call-start = ((), (), s32[]{:S(2)}) async-start(), calls=%async_computation.7 | async-start | bytes 9732096
  362.7 1.4 copy-start.4
Sparse Core Ops, SparseCore 0:
  10.6 76.7 all-gather.2
  90.0 53.5 all-gather.4
  147.4 27.3 reduce-scatter.4
  224.2 50.2 all-reduce.2
  308.9 53.7 all-reduce.4
  366.6 128.6 reduce-scatter.6
where the time goes:
time: 507 us; the launch traced here: 506 us
  waiting for transfers between devices  339 us (67%)
  blocking collectives  50.9 us (10%)
  matrix products  47.2 us (9%)
  local copies, waits for them, and re-layouts  29.4 us (6%)
  other arithmetic  20.8 us (4%)
  between operations  15.1 us (3%)
    unnamed x7, waiting for transfers between devices  130 us
    psum x2, waiting for transfers between devices, layer_backward(): lax.psum(norm_part.astype(jnp.bfloat16), 'tensor').astype(jnp.float32)  78.4 us
    all_gather x1, waiting for transfers between devices, local(): lax.all_gather(qkv_weight, 'fsdp', axis=2, tiled=True)  64.4 us
    all_gather x1, waiting for transfers between devices, local(): lax.all_gather(out_weight, 'fsdp', axis=2, tiled=True)  50.7 us
    all_gather x2, blocking collectives, layer_forward(): whole = lax.all_gather(hidden_own, 'tensor', axis=1, tiled=True)  25.5 us
    all_gather x2, blocking collectives, layer_backward(): whole_grad = lax.all_gather(grad_own, 'tensor', axis=1, tiled=True)  25.5 us
    unnamed x36, local copies, waits for them, and re-layouts  15.6 us
    dot_general x2, matrix products, layer_backward(): jnp.einsum('crh,cdh->rd', grad_qkv, w_qkv, preferred_element_type=jnp.flo...  12.7 us
  transfers between devices with their start and end apart: 8, of which 7 were waited for; matrix products, arithmetic and copies ran while one was open for 8% of the time, Pallas kernels for 0%

commit v1 on v0

--- a/solution.py
+++ b/solution.py
@@ -100,7 +100,15 @@
     live_keys = jnp.arange(length, dtype=jnp.int32)[None, :] < lengths[:, None]
     live_rows = live_keys.reshape(frame_rows, 1).astype(jnp.float32)
     gathered = (
-        lax.all_gather(qkv_weight, "fsdp", axis=2, tiled=True),
+        jnp.concatenate(
+            lax.all_to_all(
+                jnp.stack([qkv_weight for _ in range(lax.psum(1, axis_name="fsdp"))], axis=0),
+                split_axis=0,
+                concat_axis=0,
+                axis_name="fsdp",
+            ),
+            axis=2,
+        ),
         lax.all_gather(out_weight, "fsdp", axis=2, tiled=True),
     )
     w_qkv = gathered[0][0]

time: 507 us -> 566 us (1.12)
  waiting for transfers between devices: 339 us -> 377 us
  starting transfers between devices: 3.49 us -> 17.7 us
  local copies, waits for them, and re-layouts: 29.4 us -> 40.2 us
    all_to_all x0 -> x1, waiting for transfers between devices: none -> 155 us  [local(): lax.all_to_all(jnp.stack([qkv_weight for _ in range(lax.psum(1, axis_name...]
    all_gather x1 -> x0, waiting for transfers between devices: 64.4 us -> none  [local(): lax.all_gather(qkv_weight, 'fsdp', axis=2, tiled=True)]
    all_gather x1, waiting for transfers between devices: 50.7 us -> 0.02 us  [local(): lax.all_gather(out_weight, 'fsdp', axis=2, tiled=True)]
    all_to_all x0 -> x1, starting transfers between devices: none -> 12.9 us  [local(): lax.all_to_all(jnp.stack([qkv_weight for _ in range(lax.psum(1, axis_name...]
    unnamed x36 -> x38, local copies, waits for them, and re-layouts: 15.6 us -> 17.9 us
    unnamed x7 -> x6, waiting for transfers between devices: 130 us -> 130 us
  transfers between devices with their start and end apart: 8 -> 8, of which waited for: 7 -> 7; matrix products, arithmetic and copies ran while one was open for 8% -> 7% of each run, Pallas kernels for 0% -> 0%
where the time goes in v1:
time: 566 us; the launch traced here: 564 us
  waiting for transfers between devices  377 us (67%)
  blocking collectives  49.4 us (9%)
  matrix products  44.1 us (8%)
  local copies, waits for them, and re-layouts  40.2 us (7%)
  other arithmetic  20.8 us (4%)
  starting transfers between devices  17.7 us (3%)
  between operations  14.8 us (3%)
    all_to_all x1, waiting for transfers between devices, local(): lax.all_to_all(jnp.stack([qkv_weight for _ in range(lax.psum(1, axis_name...  155 us
    unnamed x6, waiting for transfers between devices  130 us
    psum x2, waiting for transfers between devices, layer_backward(): lax.psum(norm_part.astype(jnp.bfloat16), 'tensor').astype(jnp.float32)  76.5 us
    all_gather x2, blocking collectives, layer_backward(): whole_grad = lax.all_gather(grad_own, 'tensor', axis=1, tiled=True)  25.4 us
    all_gather x2, blocking collectives, layer_forward(): whole = lax.all_gather(hidden_own, 'tensor', axis=1, tiled=True)  24 us
    unnamed x38, local copies, waits for them, and re-layouts  17.9 us
    all_to_all x1, starting transfers between devices, local(): lax.all_to_all(jnp.stack([qkv_weight for _ in range(lax.psum(1, axis_name...  12.9 us
    dot_general x2, matrix products, layer_backward(): jnp.einsum('crh,cdh->rd', grad_qkv, w_qkv, preferred_element_type=jnp.flo...  12.7 us
  transfers between devices with their start and end apart: 8, of which 7 were waited for; matrix products, arithmetic and copies ran while one was open for 7% of the time, Pallas kernels for 0%

profile of v1, /device:TPU:1, one launch (start us, length us, event | category | flops | bytes accessed | tf_op | source)
XLA Modules:
  0.0 564.3 jit_solution(11762694539593623710)
XLA Ops:
  7.2 4.5 stack.18
  11.6 12.9 %all-to-all-start = ((bf16[32,1,3,96,384]{4,3,2,1,0:T(8,128)(2,1)}), bf16[32,1,3,96,384]{4,3,2,1,0:T(8,128)(2,1)}, u32[]{:S(2)}, u32[]{:S(2)}) async-start(bf16[32,1,3,96,384]{4,3,2,1,0:T(8,128)(2,1)} %stack.18), calls=%async_computation | async-start | bytes 14155776 | tf_op jit(solution)/shard_map/all_to_all | solution.py:104
  26.0 12.4 %all_gather.15 = bf16[128,3072]{1,0:T(8,128)(2,1)S(1)} all-gather(bf16[128,768]{1,0:T(8,128)(2,1)S(1)} %copy-done.8), channel_id=1, replica_groups=mesh['section'=2,'fsdp'=32,'tensor'=4] {'tensor'}, dimensions={1}, use_global_device_ids=true | all-gather | bytes 983040 | tf_op jit(solution)/shard_map/all_gather | solution.py:34
  39.0 155.2 %all-to-all-done = bf16[32,1,3,96,384]{4,3,2,1,0:T(8,128)(2,1)} async-done(((bf16[32,1,3,96,384]{4,3,2,1,0:T(8,128)(2,1)}), bf16[32,1,3,96,384]{4,3,2,1,0:T(8,128)(2,1)}, u32[]{:S(2)}, u32[]{:S(2)}) %all-to-all-start) | async-done | bytes 7077920 | tf_op jit(solution)/shard_map/all_to_all | solution.py:104
  194.2 3.9 copy.73
  202.3 3.7 fusion.10
  206.9 14.7 %all_gather.18 = bf16[128,3072]{1,0:T(8,128)(2,1)S(1)} all-gather(bf16[128,768]{1,0:T(8,128)(2,1)S(1)} %copy-done.7), channel_id=1, replica_groups=mesh['section'=2,'fsdp'=32,'tensor'=4] {'tensor'}, dimensions={1}, use_global_device_ids=true | all-gather | bytes 983040 | tf_op jit(solution)/shard_map/all_gather | solution.py:60
  221.7 12.2 %reduce-scatter.5.cloned.1.call-done = f32[128,768]{1,0:T(8,128)} async-done(((f32[128,3072]{1,0:T(8,128)}), f32[128,768]{1,0:T(8,128)}) %reduce-scatter.5.cloned.1.call-update) | async-done | bytes 393232 | tf_op jit(solution)/shard_map/reduce_scatter | solution.py:52
  235.7 3.3 collective-permute-start
  242.2 11.6 %all_gather.17 = bf16[128,3072]{1,0:T(8,128)(2,1)S(1)} all-gather(bf16[128,768]{1,0:T(8,128)(2,1)S(1)} %broadcast_select_fusion.1), channel_id=1, replica_groups=mesh['section'=2,'fsdp'=32,'tensor'=4] {'tensor'}, dimensions={1}, use_global_device_ids=true | all-gather | bytes 983040 | tf_op jit(solution)/shard_map/all_gather | solution.py:34
  254.3 4.3 fusion.22
  264.6 2.5 fusion.97
  269.1 2.1 convolution_convert_fusion.10
  271.2 2.1 convolution_convert_fusion.9
  277.6 6.4 %fusion.4 = bf16[128,3072]{1,0:T(8,128)(2,1)} fusion(bf16[3,3072,384]{2,1,0:T(8,128)(2,1)} %bitcast.130, bf16[1,128,384]{2,1,0:T(8,128)(2,1)S(1)} %copy.93, bf16[1,128,384]{2,1,0:T(8,128)(2,1)} %copy.92, bf16[1,128,384]{2,1,0:T(8,128)(2,1)} %copy.91), kind=kOutput, calls=%fused_computation.9 | convolution fusion | flops 906657792 | bytes 8159232 | tf_op jit(solution)/shard_map/crh,cdh->rd/dot_general | solution.py:83
  284.1 49.2 %all-reduce.3.cloned.1.call-done = bf16[128,3072]{1,0:T(8,128)(2,1)} async-done(((bf16[128,3072]{1,0:T(8,128)(2,1)}), bf16[128,3072]{1,0:T(8,128)(2,1)}) %all-reduce.3.cloned.1.call-update) | async-done | bytes 786448 | tf_op jit(solution)/shard_map/psum | solution.py:85
  339.6 3.5 collective-permute-done.1
  344.0 10.7 %all_gather.19 = bf16[128,3072]{1,0:T(8,128)(2,1)S(1)} all-gather(bf16[128,768]{1,0:T(8,128)(2,1)S(1)} %broadcast_select_fusion), channel_id=1, replica_groups=mesh['section'=2,'fsdp'=32,'tensor'=4] {'tensor'}, dimensions={1}, use_global_device_ids=true | all-gather | bytes 983040 | tf_op jit(solution)/shard_map/all_gather | solution.py:60
  360.9 6.2 %fusion.5 = bf16[128,3072]{1,0:T(8,128)(2,1)} fusion(bf16[3,3072,384]{2,1,0:T(8,128)(2,1)} %bitcast.131, bf16[1,128,384]{2,1,0:T(8,128)(2,1)S(1)} %copy.102, bf16[1,128,384]{2,1,0:T(8,128)(2,1)S(1)} %copy.101, bf16[1,128,384]{2,1,0:T(8,128)(2,1)S(1)} %copy.100), kind=kOutput, calls=%fused_computation.10 | convolution fusion | flops 906657792 | bytes 8159232 | tf_op jit(solution)/shard_map/crh,cdh->rd/dot_general | solution.py:83
  369.1 2.1 convolution_convert_fusion
  371.2 10.1 %pad_maximum_fusion = bf16[3072,1536]{0,1:T(8,128)(2,1)} fusion(bf16[3072,384]{0,1:T(8,128)(2,1)S(1)} %convolution_convert_fusion.1, bf16[3072,1152]{0,1:T(8,128)(2,1)S(1)} %convolution_convert_fusion), kind=kLoop, calls=%fused_computation.5 | loop fusion | flops 18874368 | bytes 18874368 | tf_op jit(solution)/shard_map/concatenate | solution.py:134
  381.4 12.6 %copy.123 = bf16[3072,1536]{1,0:T(8,128)(2,1)} copy(bf16[3072,1536]{0,1:T(8,128)(2,1)} %pad_maximum_fusion) | data formatting | bytes 18874368
  394.0 27.3 %all-reduce.5.cloned.1.call-done = bf16[128,3072]{1,0:T(8,128)(2,1)} async-done(((bf16[128,3072]{1,0:T(8,128)(2,1)}), bf16[128,3072]{1,0:T(8,128)(2,1)}) %all-reduce.5.cloned.1.call-update) | async-done | bytes 786448 | tf_op jit(solution)/shard_map/psum | solution.py:85
  425.2 128.9 %reduce-scatter.7.cloned.1.call-done = bf16[96,1536]{1,0:T(8,128)(2,1)} async-done(((bf16[3072,1536]{1,0:T(8,128)(2,1)}), bf16[96,1536]{1,0:T(8,128)(2,1)}) %reduce-scatter.7.cloned.1.call-update) | async-done | bytes 294928
  (107 shorter events, 47.0 us)
Async XLA Ops:
  11.6 14.4 %copy-start.8 = (bf16[128,768]{1,0:T(8,128)(2,1)S(1)}, bf16[128,768]{1,0:T(8,128)(2,1)}, u32[]{:S(2)}) copy-start(bf16[128,768]{1,0:T(8,128)(2,1)} %param.5) | copy-start | bytes 589828
  11.6 182.6 %all-to-all-start = ((bf16[32,1,3,96,384]{4,3,2,1,0:T(8,128)(2,1)}), bf16[32,1,3,96,384]{4,3,2,1,0:T(8,128)(2,1)}, u32[]{:S(2)}, u32[]{:S(2)}) async-start(bf16[32,1,3,96,384]{4,3,2,1,0:T(8,128)(2,1)} %stack.18), calls=%async_computation | async-start | bytes 14155776 | tf_op jit(solution)/shard_map/all_to_all | solution.py:104
  24.6 177.7 %all-gather.2.cloned.1.call-start = ((), (), s32[]{:S(2)}) async-start(), calls=%async_computation.3 | async-start | bytes 2433024 | tf_op jit(solution)/shard_map/all_gather | solution.py:112
  25.3 208.6 %reduce-scatter.5.cloned.1.call-start = ((), (), s32[]{:S(2)}) async-start(), calls=%async_computation.4 | async-start | bytes 1966080 | tf_op jit(solution)/shard_map/reduce_scatter | solution.py:52
  198.2 2.9 copy-start
  206.0 0.9 copy-start.7
  206.0 33.0 %copy-start.1 = (bf16[1,384,3072]{1,2,0:T(8,128)(2,1)S(1)}, bf16[1,384,3072]{1,2,0:T(8,128)(2,1)}, u32[]{:S(2)}) copy-start(bf16[1,384,3072]{1,2,0:T(8,128)(2,1)} %all-gather.2.cloned.1.call-done) | copy-start | bytes 7077892
  206.0 127.3 %all-reduce.3.cloned.1.call-start = ((), (), s32[]{:S(2)}) async-start(), calls=%async_computation.5 | async-start | bytes 1572864 | tf_op jit(solution)/shard_map/psum | solution.py:85
  235.7 6.4 %collective-permute-start = (bf16[128,768]{1,0:T(8,128)(2,1)}, bf16[128,768]{1,0:T(8,128)(2,1)}, u32[]{:S(2)}, u32[]{:S(2)}) collective-permute-start(bf16[128,768]{1,0:T(8,128)(2,1)} %add_convert_fusion), channel_id=1, source_target_pairs={{0,128},{1,129},{2,130},{3,131},{4,132},{5,133},{6,134},{7,135},{8... | collective-permute-start | bytes 589832 | tf_op jit(solution)/shard_map/ppermute | solution.py:13
  260.3 77.3 %copy-start.9 = (bf16[1,128,384]{1,2,0:T(8,128)(2,1)}, bf16[1,128,384]{1,2,0:T(8,128)(2,1)S(1)}, u32[]{:S(2)}) copy-start(bf16[1,128,384]{1,2,0:T(8,128)(2,1)S(1)} %copy.85) | copy-start | bytes 294916
  262.7 8.5 %copy-start.12 = (bf16[1,128,384]{1,2,0:T(8,128)(2,1)S(1)}, bf16[1,128,384]{1,2,0:T(8,128)(2,1)}, u32[]{:S(2)}) copy-start(bf16[1,128,384]{1,2,0:T(8,128)(2,1)} %copy.81) | copy-start | bytes 294916
  284.1 137.3 %all-reduce.5.cloned.1.call-start = ((), (), s32[]{:S(2)}) async-start(), calls=%async_computation.6 | async-start | bytes 1572864 | tf_op jit(solution)/shard_map/psum | solution.py:85
  333.3 1.8 copy-start.6
  335.1 1.2 copy-start.4
  335.2 2.5 copy-start.13
  336.3 6.7 %collective-permute-start.1 = (bf16[128,768]{1,0:T(8,128)(2,1)}, bf16[128,768]{1,0:T(8,128)(2,1)}, u32[]{:S(2)}, u32[]{:S(2)}) collective-permute-start(bf16[128,768]{1,0:T(8,128)(2,1)} %fusion.54), channel_id=1, source_target_pairs={{128,0},{129,1},{130,2},{131,3},{132,4},{133,5},{134,6},{135,7},{1... | collective-permute-start | bytes 589832 | tf_op jit(solution)/shard_map/ppermute | solution.py:13
  355.6 2.2 copy-start.10
  356.2 1.8 copy-start.15
  356.2 1.8 copy-start.16
  356.2 3.0 copy-start.14
  367.2 1.1 copy-start.3
  367.2 1.1 copy-start.11
  367.5 186.6 %reduce-scatter.7.cloned.1.call-start = ((), (), s32[]{:S(2)}) async-start(), calls=%async_computation.7 | async-start | bytes 9732096
  421.3 1.4 copy-start.5
  (1 other events, 0.9 us)
Sparse Core Ops, SparseCore 0:
  28.0 102.6 all-gather.1
  206.2 27.6 reduce-scatter.4
  284.2 49.0 all-reduce.2
  367.6 53.7 all-reduce.4
  425.2 128.7 reduce-scatter.6
